TPU v7x, 128 devices: a whole 4x4x4 slice. The times are simulated.
128 devices in a mesh: section: 8 (over z, x_lo), dp: 16 (over y, x_hi, core).
Axes of the slice: x: 4 (x_hi: 2, x_lo: 2; x = x_hi * 2 + x_lo), y: 4, z: 4, core: 2. Of those that a mesh axis runs over, the one named last changes fastest.
Arguments:
- master: float32 [8, 2560, 2560], P('section', 'dp'), may hold values from -0.125 to 0.125
- first_moment: float32 [8, 2560, 2560], P('section', 'dp'), may hold values from -3 to 3
- second_moment: float32 [8, 2560, 2560], P('section', 'dp'), may hold values from 0.1 to 4
- inputs_own: bfloat16 [8, 4, 2048, 2560], P('section', None, 'dp'), may hold values from -6 to 6
- inputs_arriving: bfloat16 [8, 4, 2048, 2560], P('section', None, 'dp'), may hold values from -6 to 6
- grads_own: bfloat16 [8, 4, 2048, 2560], P('section', None, 'dp'), may hold values from -0.13183594 to 0.13183594
- windows_own: int32 [8, 2048, 2560], P('section', 'dp'), may hold values from 0 to 15
- windows_arriving: int32 [8, 2048, 2560], P('section', 'dp'), may hold values from 0 to 15
- next_inputs: bfloat16 [8, 512, 2560], P('section', 'dp'), may hold values from -6 to 6
Outputs:
- fresh_params: float32 [8, 2560, 2560], P('section', 'dp')
- fresh_first: float32 [8, 2560, 2560], P('section', 'dp')
- fresh_second: float32 [8, 2560, 2560], P('section', 'dp')
- next_currents: bfloat16 [8, 512, 2560], P('section', 'dp')
Inputs may be any that keep to these rules, and one draw needn't show every extreme that they name: `windows_own`: bit t of an entry is the surrogate derivative of spikes_t by v_t for timestep t. `windows_arriving`: bit t of an entry is the surrogate derivative of spikes_t by v_t for timestep t.
All inputs are finite; a program needn't handle non-finite values.
Results may differ from a plain program's by a relative error of at most 0.008.
Values may be sent and summed in bfloat16 or wider, within the bound.
A program may use at most 128 MiB of HBM per device.

v0:
```python
import jax
import jax.numpy as jnp
from jax import lax
from jax.sharding import PartitionSpec as P

LEAK_RATE = 0.5
LEARN_RATE = 0.002
FIRST_DECAY = 0.9
SECOND_DECAY = 0.95
EPSILON = 1e-08
WEIGHT_DECAY = 0.1
FIRST_CORRECTION = 1.0 - 0.9**10
SECOND_CORRECTION = 1.0 - 0.95**10


def passed_along(shard, axis, by):
    count = lax.axis_size(axis)
    pairs = [(i, i + by) for i in range(count) if 0 <= i + by < count]
    return lax.ppermute(shard, axis, pairs)


def membrane_grads(gradients, windows):
    carried = jnp.zeros(gradients.shape[1:], jnp.float32)
    results = []
    for moment in reversed(range(gradients.shape[0])):
        window = jnp.bitwise_and(jnp.right_shift(windows, moment), 1).astype(jnp.float32)
        carried = window * gradients[moment].astype(jnp.float32) + LEAK_RATE * carried
        results = [carried] + results
    return jnp.stack(results).astype(jnp.bfloat16)


def shards(
    master,
    first_moment,
    second_moment,
    inputs_own,
    inputs_arriving,
    grads_own,
    windows_own,
    windows_arriving,
    next_inputs,
):
    params = master[0]
    timesteps, tok_rows, features = (grads_own.shape[1], grads_own.shape[2], grads_own.shape[3])
    flat_rows = timesteps * tok_rows
    membrane_own = membrane_grads(grads_own[0], windows_own[0]).reshape(flat_rows, features)
    through = lax.dot_general(
        membrane_own,
        lax.all_gather(params.astype(jnp.bfloat16), "dp", axis=0, tiled=True),
        (((1,), (1,)), ((), ())),
        preferred_element_type=jnp.float32,
    )
    outgoing = (grads_own[0].reshape(flat_rows, features).astype(jnp.float32) + through).astype(
        jnp.bfloat16
    )
    received = passed_along(outgoing.reshape(timesteps, tok_rows, features), "section", -1)
    membrane_arriving = membrane_grads(received, windows_arriving[0]).reshape(flat_rows, features)
    acts_own = inputs_own[0].reshape(flat_rows, features)
    acts_arriving = inputs_arriving[0].reshape(flat_rows, features)
    contract = (((0,), (0,)), ((), ()))
    partial_value = lax.dot_general(
        acts_own, membrane_own, contract, preferred_element_type=jnp.float32
    )
    gradient = lax.psum_scatter(
        (
            partial_value
            + lax.dot_general(
                acts_arriving, membrane_arriving, contract, preferred_element_type=jnp.float32
            )
        ).astype(jnp.bfloat16),
        "dp",
        scatter_dimension=0,
        tiled=True,
    ).astype(jnp.float32)
    fresh_first = FIRST_DECAY * first_moment[0] + (1.0 - FIRST_DECAY) * gradient
    fresh_second = SECOND_DECAY * second_moment[0] + (1.0 - SECOND_DECAY) * gradient * gradient
    direction = (
        fresh_first / FIRST_CORRECTION / (jnp.sqrt(fresh_second / SECOND_CORRECTION) + EPSILON)
    )
    fresh_params = params - LEARN_RATE * (direction + WEIGHT_DECAY * params)
    fresh_weights = fresh_params.astype(jnp.bfloat16)
    upcoming = next_inputs[0]
    currents = jnp.dot(
        upcoming,
        lax.all_gather(fresh_weights, "dp", axis=0, tiled=True),
        preferred_element_type=jnp.float32,
    )
    next_currents = currents.astype(jnp.bfloat16)
    return (fresh_params[None], fresh_first[None], fresh_second[None], next_currents[None])


def solution(mesh):
    return jax.shard_map(
        shards,
        mesh=mesh,
        in_specs=(
            P("section", "dp", None),
            P("section", "dp", None),
            P("section", "dp", None),
            P("section", None, "dp", None),
            P("section", None, "dp", None),
            P("section", None, "dp", None),
            P("section", "dp", None),
            P("section", "dp", None),
            P("section", "dp", None),
        ),
        out_specs=(
            P("section", "dp", None),
            P("section", "dp", None),
            P("section", "dp", None),
            P("section", "dp", None),
        ),
        check_vma=False,
    )
```

profile of v0, /device:TPU:1, one launch (start us, length us, event | category | flops | bytes accessed | tf_op | source)
XLA Modules:
  0.0 454.4 jit_solution(939705589628608496)
XLA Ops:
  7.2 0.0 copy-start
  7.2 0.0 all-gather.3.cloned.1.call-start
  7.2 2.6 bitcast_convert_fusion
  9.8 0.0 all-gather.3.cloned.1.call-update
  9.8 0.0 reduce-scatter.4.cloned.1.call-start
  9.9 3.2 fusion.9
  13.1 1.8 maximum_convert_fusion
  14.9 92.3 %all-gather.3.cloned.1.call-done = bf16[2560,2560]{1,0:T(8,128)(2,1)} async-done(((bf16[160,2560]{1,0:T(8,128)(2,1)}), bf16[2560,2560]{1,0:T(8,128)(2,1)}) %all-gather.3.cloned.1.call-update) | async-done | bytes 13107216 | tf_op jit(solution)/shard_map/all_gather | solution.py:49
  107.2 0.0 copy-start.3
  107.2 13.9 %fusion.1 = bf16[512,2560]{1,0:T(8,128)(2,1)} fusion(bf16[512,2560]{1,0:T(8,128)(2,1)} %bitcast.79, bf16[512,2560]{1,0:T(8,128)(2,1)} %bitcast.80, bf16[2560,2560]{1,0:T(8,128)(2,1)} %all-gather.3.cloned.1.call-done), kind=kOutput, calls=%fused_computation.4 | convolution fusion | flops 6714818560 | bytes 20971520 | tf_op jit(solution)/shard_map/dot_general | solution.py:47
  121.1 1.5 collective-permute-start
  122.6 0.0 copy-done
  122.6 0.0 copy-done.3
  122.6 0.0 copy-start.4
  122.6 12.3 %fusion.17 = f32[2560,2560]{1,0:T(8,128)} fusion(bf16[512,2560]{1,0:T(8,128)(2,1)S(1)} %bitcast.81, bf16[512,2560]{1,0:T(8,128)(2,1)S(1)} %bitcast.78), kind=kOutput, calls=%fused_computation.35 | convolution fusion | flops 6710886400 | bytes 31457280 | tf_op jit(solution)/shard_map/dot_general | solution.py:61
  134.9 46.4 %collective-permute-done = bf16[4,128,2560]{2,1,0:T(8,128)(2,1)S(1)} collective-permute-done((bf16[4,128,2560]{2,1,0:T(8,128)(2,1)}, bf16[4,128,2560]{2,1,0:T(8,128)(2,1)S(1)}, u32[]{:S(2)}, u32[]{:S(2)}) %collective-permute-start) | collective-permute-done | bytes 2621472 | tf_op jit(solution)/shard_map/ppermute | solution.py:19
  181.4 0.0 copy-done.4
  181.4 1.2 add_convert_fusion.1
  182.5 1.8 pad_maximum_fusion
  184.4 16.4 %fusion = bf16[2560,2560]{0,1:T(8,128)(2,1)} fusion(f32[2560,2560]{1,0:T(8,128)} %fusion.17, bf16[512,2560]{1,0:T(8,128)(2,1)} %bitcast.82, bf16[512,2560]{1,0:T(8,128)(2,1)} %bitcast.84), kind=kOutput, calls=%fused_computation.1 | convolution fusion | flops 6723993600 | bytes 44564480 | tf_op jit(solution)/shard_map/dot_general | solution.py:67
  200.8 17.7 %copy.20 = bf16[2560,2560]{1,0:T(8,128)(2,1)} copy(bf16[2560,2560]{0,1:T(8,128)(2,1)} %fusion) | data formatting | bytes 26214400
  218.4 0.0 copy-start.2
  218.4 0.0 reduce-scatter.4.cloned.1.call-update
  218.5 0.0 copy-start.5
  218.5 0.0 all-gather.5.cloned.1.call-start
  218.5 123.0 %reduce-scatter.4.cloned.1.call-done = bf16[160,2560]{1,0:T(8,128)(2,1)} async-done(((bf16[2560,2560]{1,0:T(8,128)(2,1)}), bf16[160,2560]{1,0:T(8,128)(2,1)}) %reduce-scatter.4.cloned.1.call-update) | async-done | bytes 819216 | tf_op jit(solution)/shard_map/reduce_scatter | solution.py:64
  341.5 0.0 copy-done.2
  341.5 6.0 %fusion.16 = (bf16[160,2560]{1,0:T(8,128)(2,1)}, f32[160,2560]{1,0:T(8,128)}, f32[1,160,2560]{2,1,0:T(8,128)}, f32[1,160,2560]{2,1,0:T(8,128)}) fusion(f32[1,160,2560]{2,1,0:T(8,128)} %param.11, bf16[160,2560]{1,0:T(8,128)(2,1)} %reduce-scatter.4.cloned.1.call-done, f32[1,160,2560]{2,1,0:T(8,128)} %param.10, f32[1,160,2560]{2,1,0:T(8,128)S(1)} %copy-done.2), kind=kLoop, calls=%fused_computation.34 | loop fusion | flops 6963200 | bytes 11468800 | tf_op jit(solution)/shard_map/convert_element_type | solution.py:81
  347.5 0.0 all-gather.5.cloned.1.call-update
  347.5 92.4 %all-gather.5.cloned.1.call-done = bf16[2560,2560]{1,0:T(8,128)(2,1)} async-done(((bf16[160,2560]{1,0:T(8,128)(2,1)}), bf16[2560,2560]{1,0:T(8,128)(2,1)}) %all-gather.5.cloned.1.call-update) | async-done | bytes 13107216 | tf_op jit(solution)/shard_map/all_gather | solution.py:85
  439.9 0.0 copy-done.5
  439.9 0.0 copy-start.1
  439.9 7.9 %fusion.2 = bf16[1,32,2560]{2,1,0:T(8,128)(2,1)} fusion(bf16[2560,2560]{1,0:T(8,128)(2,1)} %all-gather.5.cloned.1.call-done, bf16[1,32,2560]{2,1,0:T(8,128)(2,1)S(1)} %copy-done.5), kind=kOutput, calls=%fused_computation.6 | convolution fusion | flops 419512320 | bytes 13434880 | tf_op jit(solution)/shard_map/dot_general | solution.py:83
  447.8 0.0 copy-done.1
Async XLA Ops:
  7.2 115.4 %copy-start = (bf16[1,4,128,2560]{3,2,1,0:T(8,128)(2,1)S(1)}, bf16[1,4,128,2560]{3,2,1,0:T(8,128)(2,1)}, u32[]{:S(2)}) copy-start(bf16[1,4,128,2560]{3,2,1,0:T(8,128)(2,1)} %param.12) | copy-start | bytes 7864324
  7.2 100.0 %all-gather.3.cloned.1.call-start = ((), (), s32[]{:S(2)}) async-start(), calls=%async_computation.1 | async-start | bytes 13926400 | tf_op jit(solution)/shard_map/all_gather | solution.py:49
  9.8 331.7 %reduce-scatter.4.cloned.1.call-start = ((), (), s32[]{:S(2)}) async-start(), calls=%async_computation.3 | async-start | bytes 13926400 | tf_op jit(solution)/shard_map/reduce_scatter | solution.py:64
  107.2 15.4 %copy-start.3 = (bf16[4,128,2560]{2,1,0:T(8,128)(2,1)S(1)}, bf16[4,128,2560]{2,1,0:T(8,128)(2,1)}, u32[]{:S(2)}) copy-start(bf16[4,128,2560]{2,1,0:T(8,128)(2,1)} %maximum_convert_fusion) | copy-start | bytes 7864324
  121.1 60.3 %collective-permute-start = (bf16[4,128,2560]{2,1,0:T(8,128)(2,1)}, bf16[4,128,2560]{2,1,0:T(8,128)(2,1)S(1)}, u32[]{:S(2)}, u32[]{:S(2)}) collective-permute-start(bf16[4,128,2560]{2,1,0:T(8,128)(2,1)} %bitcast.85), channel_id=1, source_target_pairs={{16,0},{32,16},{48,32},{64,48},{80,64},{96,80},{112,96},{17,1},{33... | collective-permute-start | bytes 7864328 | tf_op jit(solution)/shard_map/ppermute | solution.py:19
  122.6 58.8 %copy-start.4 = (s32[1,128,2560]{2,1,0:T(8,128)S(1)}, s32[1,128,2560]{2,1,0:T(8,128)}, u32[]{:S(2)}) copy-start(s32[1,128,2560]{2,1,0:T(8,128)} %param.16) | copy-start | bytes 3932164
  218.4 123.1 %copy-start.2 = (f32[1,160,2560]{2,1,0:T(8,128)S(1)}, f32[1,160,2560]{2,1,0:T(8,128)}, u32[]{:S(2)}) copy-start(f32[1,160,2560]{2,1,0:T(8,128)} %param.9) | copy-start | bytes 4915204
  218.5 221.5 %copy-start.5 = (bf16[1,32,2560]{2,1,0:T(8,128)(2,1)S(1)}, bf16[1,32,2560]{2,1,0:T(8,128)(2,1)}, u32[]{:S(2)}) copy-start(bf16[1,32,2560]{2,1,0:T(8,128)(2,1)} %param.17) | copy-start | bytes 491524
  218.5 221.5 %all-gather.5.cloned.1.call-start = ((), (), s32[]{:S(2)}) async-start(), calls=%async_computation.2 | async-start | bytes 13926400 | tf_op jit(solution)/shard_map/all_gather | solution.py:85
  439.9 7.9 %copy-start.1 = (bf16[1,4,128,2560]{3,2,1,0:T(8,128)(2,1)S(1)}, bf16[1,4,128,2560]{3,2,1,0:T(8,128)(2,1)}, u32[]{:S(2)}) copy-start(bf16[1,4,128,2560]{3,2,1,0:T(8,128)(2,1)} %param.12) | copy-start | bytes 7864324
Sparse Core Ops, SparseCore 0:
  11.0 96.1 all-gather.2
  218.6 122.9 reduce-scatter.3
  347.7 92.2 all-gather.4
where the time goes:
time: 455 us; the launch traced here: 454 us
  waiting for transfers between devices  354 us (78%)
  matrix products  50.5 us (11%)
  local copies, waits for them, and re-layouts  17.7 us (4%)
  other arithmetic  16.5 us (4%)
  between operations  13.8 us (3%)
    reduce_scatter x1, waiting for transfers between devices, shards(): lax.psum_scatter((partial_value + lax.dot_general(acts_arriving, membrane...  123 us
    all_gather x1, waiting for transfers between devices, shards(): lax.all_gather(fresh_weights, 'dp', axis=0, tiled=True)  92.4 us
    all_gather x1, waiting for transfers between devices, shards(): lax.all_gather(params.astype(jnp.bfloat16), 'dp', axis=0, tiled=True)  92.3 us
    ppermute x1, waiting for transfers between devices, passed_along(): return lax.ppermute(shard, axis, pairs)  46.4 us
    unnamed x13, local copies, waits for them, and re-layouts  17.7 us
    dot_general x1, matrix products, shards(): lax.dot_general(acts_arriving, membrane_arriving, contract, preferred_ele...  16.4 us
    dot_general x1, matrix products, shards(): lax.dot_general(membrane_own, lax.all_gather(params.astype(jnp.bfloat16),...  13.9 us
    dot_general x1, matrix products, shards(): lax.dot_general(acts_own, membrane_own, contract, preferred_element_type=...  12.3 us
  transfers between devices with their start and end apart: 4, of which 4 were waited for; matrix products, arithmetic and copies ran while one was open for 4% of the time, Pallas kernels for 0%

commit v1 on v0

--- a/solution.py
+++ b/solution.py
@@ -46,7 +46,15 @@
     membrane_own = membrane_grads(grads_own[0], windows_own[0]).reshape(flat_rows, features)
     through = lax.dot_general(
         membrane_own,
-        lax.all_gather(params.astype(jnp.bfloat16), "dp", axis=0, tiled=True),
+        jnp.concatenate(
+            lax.all_to_all(
+                jnp.stack([params.astype(jnp.bfloat16)] * lax.axis_size("dp"), 0),
+                axis_name="dp",
+                concat_axis=0,
+                split_axis=0,
+            ),
+            axis=0,
+        ),
         (((1,), (1,)), ((), ())),
         preferred_element_type=jnp.float32,
     )

time: 455 us -> 526 us (1.16)
  waiting for transfers between devices: 354 us -> 387 us
  local copies, waits for them, and re-layouts: 17.7 us -> 44.5 us
  starting transfers between devices: 1.58 us -> 10.2 us
    all_to_all x0 -> x1, waiting for transfers between devices: none -> 141 us  [shards(): lax.all_to_all(jnp.stack([params.astype(jnp.bfloat16)] * lax.axis_size('d...]
    reduce_scatter x1 -> x0, waiting for transfers between devices: 123 us -> none  [shards(): lax.psum_scatter((partial_value + lax.dot_general(acts_arriving, membrane...]
    unnamed x3, waiting for transfers between devices: 0.05 us -> 116 us
    all_gather x1 -> x0, waiting for transfers between devices: 92.3 us -> none  [shards(): lax.all_gather(params.astype(jnp.bfloat16), 'dp', axis=0, tiled=True)]
    unnamed x13 -> x22, local copies, waits for them, and re-layouts: 17.7 us -> 36.2 us
    all_to_all x0 -> x1, starting transfers between devices: none -> 8.44 us  [shards(): lax.all_to_all(jnp.stack([params.astype(jnp.bfloat16)] * lax.axis_size('d...]
    all_gather x1, waiting for transfers between devices: 92.4 us -> 84.6 us  [shards(): lax.all_gather(fresh_weights, 'dp', axis=0, tiled=True)]
    another operation x0 -> x1, local copies, waits for them, and re-layouts: none -> 6.01 us  [shards(): jnp.stack([params.astype(jnp.bfloat16)] * lax.axis_size('dp'), 0)]
  transfers between devices with their start and end apart: 4 -> 4, of which waited for: 4 -> 4; matrix products, arithmetic and copies ran while one was open for 4% -> 6% of each run, Pallas kernels for 0% -> 0%
where the time goes in v1:
time: 526 us; the launch traced here: 525 us
  waiting for transfers between devices  387 us (74%)
  matrix products  50.5 us (10%)
  local copies, waits for them, and re-layouts  44.5 us (8%)
  other arithmetic  18.3 us (3%)
  between operations  14.1 us (3%)
  starting transfers between devices  10.2 us (2%)
    all_to_all x1, waiting for transfers between devices, shards(): lax.all_to_all(jnp.stack([params.astype(jnp.bfloat16)] * lax.axis_size('d...  141 us
    unnamed x3, waiting for transfers between devices  116 us
    all_gather x1, waiting for transfers between devices, shards(): lax.all_gather(fresh_weights, 'dp', axis=0, tiled=True)  84.6 us
    ppermute x1, waiting for transfers between devices, passed_along(): return lax.ppermute(shard, axis, pairs)  45.7 us
    unnamed x22, local copies, waits for them, and re-layouts  36.2 us
    dot_general x1, matrix products, shards(): lax.dot_general(acts_arriving, membrane_arriving, contract, preferred_ele...  16.4 us
    dot_general x1, matrix products, shards(): lax.dot_general(membrane_own, jnp.concatenate(lax.all_to_all(jnp.stack([p...  13.9 us
    dot_general x1, matrix products, shards(): lax.dot_general(acts_own, membrane_own, contract, preferred_element_type=...  12.3 us
  transfers between devices with their start and end apart: 4, of which 4 were waited for; matrix products, arithmetic and copies ran while one was open for 6% of the time, Pallas kernels for 0%

profile of v1, /device:TPU:1, one launch (start us, length us, event | category | flops | bytes accessed | tf_op | source)
XLA Modules:
  0.0 525.0 jit_solution(12614165933850158711)
XLA Ops:
  7.2 0.0 copy-start
  7.2 1.7 convert_bitcast_fusion
  8.9 6.0 %stack.12 = bf16[16,160,2560]{2,1,0:T(8,128)(2,1)} broadcast(bf16[160,2560]{1,0:T(8,128)(2,1)S(1)} %convert_bitcast_fusion), dimensions={1,2} | broadcast | bytes 13926400 | tf_op jit(solution)/shard_map/stack | solution.py:51
  14.9 8.4 %all-to-all-start = ((bf16[16,160,2560]{2,1,0:T(8,128)(2,1)}), bf16[16,160,2560]{2,1,0:T(8,128)(2,1)}, u32[]{:S(2)}, u32[]{:S(2)}) async-start(bf16[16,160,2560]{2,1,0:T(8,128)(2,1)} %stack.12), calls=%async_computation | async-start | bytes 26214400 | tf_op jit(solution)/shard_map/all_to_all | solution.py:50
  23.3 0.0 reduce-scatter.4.cloned.1.call-start
  23.3 3.2 fusion.12
  26.6 1.8 pad_maximum_fusion
  28.4 141.4 %all-to-all-done = bf16[16,160,2560]{2,1,0:T(8,128)(2,1)} async-done(((bf16[16,160,2560]{2,1,0:T(8,128)(2,1)}), bf16[16,160,2560]{2,1,0:T(8,128)(2,1)}, u32[]{:S(2)}, u32[]{:S(2)}) %all-to-all-start) | async-done | bytes 13107232 | tf_op jit(solution)/shard_map/all_to_all | solution.py:50
  169.7 0.0 copy-start.3
  169.7 13.9 %fusion.1 = bf16[512,2560]{1,0:T(8,128)(2,1)} fusion(bf16[512,2560]{1,0:T(8,128)(2,1)} %bitcast.85, bf16[512,2560]{1,0:T(8,128)(2,1)} %bitcast.86, bf16[2560,2560]{1,0:T(8,128)(2,1)} %bitcast.10), kind=kOutput, calls=%fused_computation.3 | convolution fusion | flops 6714818560 | bytes 20971520 | tf_op jit(solution)/shard_map/dot_general | solution.py:47
  183.6 1.5 collective-permute-start
  185.1 0.0 copy-done
  185.1 0.0 copy-done.3
  185.1 0.0 copy-start.5
  185.1 12.3 %fusion.21 = f32[2560,2560]{1,0:T(8,128)} fusion(bf16[512,2560]{1,0:T(8,128)(2,1)S(1)} %bitcast.87, bf16[512,2560]{1,0:T(8,128)(2,1)S(1)} %bitcast.83), kind=kOutput, calls=%fused_computation.39 | convolution fusion | flops 6710886400 | bytes 31457280 | tf_op jit(solution)/shard_map/dot_general | solution.py:69
  197.4 45.7 %collective-permute-done = bf16[4,128,2560]{2,1,0:T(8,128)(2,1)S(1)} collective-permute-done((bf16[4,128,2560]{2,1,0:T(8,128)(2,1)}, bf16[4,128,2560]{2,1,0:T(8,128)(2,1)S(1)}, u32[]{:S(2)}, u32[]{:S(2)}) %collective-permute-start) | collective-permute-done | bytes 2621472 | tf_op jit(solution)/shard_map/ppermute | solution.py:19
  243.1 0.0 copy-done.5
  243.1 1.2 add_convert_fusion.1
  244.3 1.8 pad_maximum_fusion.1
  246.1 16.4 %fusion = bf16[2560,2560]{0,1:T(8,128)(2,1)} fusion(f32[2560,2560]{1,0:T(8,128)} %fusion.21, bf16[512,2560]{1,0:T(8,128)(2,1)} %bitcast.88, bf16[512,2560]{1,0:T(8,128)(2,1)} %bitcast.89), kind=kOutput, calls=%fused_computation.1 | convolution fusion | flops 6723993600 | bytes 44564480 | tf_op jit(solution)/shard_map/dot_general | solution.py:75
  262.5 17.7 %copy.26 = bf16[2560,2560]{1,0:T(8,128)(2,1)} copy(bf16[2560,2560]{0,1:T(8,128)(2,1)} %fusion) | data formatting | bytes 26214400
  280.2 0.0 copy-start.2
  280.2 0.0 reduce-scatter.4.cloned.1.call-update
  280.2 0.3 all-gather.2.cloned.1.call-start
  280.5 1.1 copy-done.2
  281.6 2.0 copy.19
  283.6 0.0 copy-start.4
  283.6 3.2 copy.20
  286.8 0.0 copy-done.4
  286.8 2.0 copy.21
  288.8 115.7 %reduce-scatter.4.cloned.1.call-done = bf16[160,2560]{1,0:T(8,128)(2,1)} async-done(((bf16[2560,2560]{1,0:T(8,128)(2,1)}), bf16[160,2560]{1,0:T(8,128)(2,1)}) %reduce-scatter.4.cloned.1.call-update) | async-done | bytes 819216
  404.6 2.3 copy.27
  406.9 8.6 %fusion.20 = (bf16[160,2560]{0,1:T(8,128)(2,1)}, f32[160,2560]{0,1:T(8,128)}, f32[1,160,2560]{1,2,0:T(8,128)S(1)}, f32[1,160,2560]{1,2,0:T(8,128)}) fusion(f32[1,160,2560]{1,2,0:T(8,128)} %copy.21, bf16[160,2560]{0,1:T(8,128)(2,1)} %copy.27, f32[1,160,2560]{1,2,0:T(8,128)} %copy.20, f32[1,160,2560]{1,2,0:T(8,128)} %copy.19), kind=kLoop, calls=%fused_computation.38 | loop fusion | flops 6963200 | bytes 11468800 | tf_op jit(solution)/shard_map/convert_element_type | solution.py:89
  415.5 2.3 copy.22
  417.8 0.0 all-gather.2.cloned.1.call-update
  417.8 3.0 copy.23
  420.8 3.0 copy.24
  423.8 0.0 copy-start.6
  423.8 1.8 copy.25
  425.6 84.6 %all-gather.2.cloned.1.call-done = bf16[2560,2560]{1,0:T(8,128)(2,1)} async-done(((bf16[160,2560]{1,0:T(8,128)(2,1)}), bf16[2560,2560]{1,0:T(8,128)(2,1)}) %all-gather.2.cloned.1.call-update) | async-done | bytes 13107216 | tf_op jit(solution)/shard_map/all_gather | solution.py:93
  510.3 0.0 copy-done.6
  510.3 0.0 copy-start.1
  510.3 7.9 %fusion.2 = bf16[1,32,2560]{2,1,0:T(8,128)(2,1)} fusion(bf16[2560,2560]{1,0:T(8,128)(2,1)} %all-gather.2.cloned.1.call-done, bf16[1,32,2560]{2,1,0:T(8,128)(2,1)S(1)} %copy-done.6), kind=kOutput, calls=%fused_computation.6 | convolution fusion | flops 419512320 | bytes 13434880 | tf_op jit(solution)/shard_map/dot_general | solution.py:91
  518.1 0.0 copy-done.1
Async XLA Ops:
  7.2 177.9 %copy-start = (bf16[1,4,128,2560]{3,2,1,0:T(8,128)(2,1)S(1)}, bf16[1,4,128,2560]{3,2,1,0:T(8,128)(2,1)}, u32[]{:S(2)}) copy-start(bf16[1,4,128,2560]{3,2,1,0:T(8,128)(2,1)} %param.12) | copy-start | bytes 7864324
  14.9 154.9 %all-to-all-start = ((bf16[16,160,2560]{2,1,0:T(8,128)(2,1)}), bf16[16,160,2560]{2,1,0:T(8,128)(2,1)}, u32[]{:S(2)}, u32[]{:S(2)}) async-start(bf16[16,160,2560]{2,1,0:T(8,128)(2,1)} %stack.12), calls=%async_computation | async-start | bytes 26214400 | tf_op jit(solution)/shard_map/all_to_all | solution.py:50
  23.3 381.3 %reduce-scatter.4.cloned.1.call-start = ((), (), s32[]{:S(2)}) async-start(), calls=%async_computation.3 | async-start | bytes 13926400
  169.7 15.4 %copy-start.3 = (bf16[4,128,2560]{2,1,0:T(8,128)(2,1)S(1)}, bf16[4,128,2560]{2,1,0:T(8,128)(2,1)}, u32[]{:S(2)}) copy-start(bf16[4,128,2560]{2,1,0:T(8,128)(2,1)} %pad_maximum_fusion) | copy-start | bytes 7864324
  183.6 59.5 %collective-permute-start = (bf16[4,128,2560]{2,1,0:T(8,128)(2,1)}, bf16[4,128,2560]{2,1,0:T(8,128)(2,1)S(1)}, u32[]{:S(2)}, u32[]{:S(2)}) collective-permute-start(bf16[4,128,2560]{2,1,0:T(8,128)(2,1)} %bitcast.90), channel_id=1, source_target_pairs={{16,0},{32,16},{48,32},{64,48},{80,64},{96,80},{112,96},{17,1},{33... | collective-permute-start | bytes 7864328 | tf_op jit(solution)/shard_map/ppermute | solution.py:19
  185.1 58.0 %copy-start.5 = (s32[1,128,2560]{2,1,0:T(8,128)S(1)}, s32[1,128,2560]{2,1,0:T(8,128)}, u32[]{:S(2)}) copy-start(s32[1,128,2560]{2,1,0:T(8,128)} %param.16) | copy-start | bytes 3932164
  280.2 1.4 copy-start.2
  280.2 230.1 %all-gather.2.cloned.1.call-start = ((), (), s32[]{:S(2)}) async-start(), calls=%async_computation.2 | async-start | bytes 13926400 | tf_op jit(solution)/shard_map/all_gather | solution.py:93
  283.6 3.2 copy-start.4
  423.8 86.4 %copy-start.6 = (bf16[1,32,2560]{2,1,0:T(8,128)(2,1)S(1)}, bf16[1,32,2560]{2,1,0:T(8,128)(2,1)}, u32[]{:S(2)}) copy-start(bf16[1,32,2560]{2,1,0:T(8,128)(2,1)} %param.17) | copy-start | bytes 491524
  510.3 7.9 %copy-start.1 = (bf16[1,4,128,2560]{3,2,1,0:T(8,128)(2,1)S(1)}, bf16[1,4,128,2560]{3,2,1,0:T(8,128)(2,1)}, u32[]{:S(2)}) copy-start(bf16[1,4,128,2560]{3,2,1,0:T(8,128)(2,1)} %param.12) | copy-start | bytes 7864324
Sparse Core Ops, SparseCore 0:
  280.3 124.2 reduce-scatter.3
  418.0 92.2 all-gather.1
